TPU v7x, 32 devices: a whole 2x2x4 slice. The times are simulated.
32 devices in a mesh: row: 4 (over x, core), col: 8 (over z, y).
Axes of the slice: x: 2, y: 2, z: 4, core: 2. Of those that a mesh axis runs over, the one named last changes fastest.
Arguments:
- rhs: float32 [32768, 512], P('col', 'row'), may hold values from -6 to 6
- factors: bfloat16 [32768, 2048], P('col', 'row'), may hold values from -0.15625 to 0.15625
- diag_inv: float32 [4, 512, 512], replicated, may hold values from -2 to 2, as said below
Outputs:
- solution: float32 [32768, 512], P('col', 'row')
Inputs may be any that keep to these rules, and one draw needn't show every extreme that they name: `diag_inv`: entries off the diagonal of each block lie within 2 / sqrt(512) in magnitude; diagonal entries lie in 0.5 to 2.
All inputs are finite; a program needn't handle non-finite values.
Results may differ from a plain program's by a relative error of at most 0.0038.
Values may be sent and summed in bfloat16 or wider, within the bound.
A program may use at most 128 MiB of HBM per device.

v0:
```python
import jax
import jax.numpy as jnp
from jax import lax
from jax.sharding import PartitionSpec as P


def body(rhs, factors, diag_inv):
    rows_dev = rhs.shape[0]
    steps = diag_inv.shape[0]
    block = diag_inv.shape[1]
    col_count = lax.axis_size("col")
    block_span = rows_dev * col_count // steps
    my_index = lax.axis_index("col")
    global_rows = my_index * rows_dev + jnp.arange(rows_dev)
    index = jnp.arange(block)
    strict_lower = index[:, None] > index[None, :]
    eye = jnp.eye(block, dtype=jnp.float32)
    panel_rows = lax.all_gather(factors, "row", axis=1, tiled=True)

    def solve_block(matrix, work, step):
        owner_index = step * col_count // steps
        owner = my_index == owner_index
        product = jnp.dot(
            matrix,
            work[:block],
            precision=lax.Precision.HIGHEST,
            preferred_element_type=jnp.float32,
        )
        solved = lax.psum(jnp.where(owner, product, jnp.float32(0.0)), "col")
        return (solved, owner)

    def apply_update(work, solved, owner, columns, row_mask):
        product = jnp.dot(columns, solved.astype(jnp.bfloat16), preferred_element_type=jnp.float32)
        updated = jnp.where(row_mask[:, None], work - product, work)
        leading = jnp.where(owner, solved, updated[:block])
        return jnp.concatenate([leading, updated[block:]], axis=0)

    work = rhs
    kept_columns = []
    for step in range(steps):
        lower_inv = jnp.where(strict_lower, diag_inv[step], jnp.float32(0.0)) + eye
        solved, owner = solve_block(lower_inv, work, step)
        columns = panel_rows[:, step * block : (step + 1) * block]
        kept_columns.append(columns)
        row_mask = global_rows >= step * block_span + block
        work = apply_update(work, solved, owner, columns, row_mask)
    for step in reversed(range(steps)):
        upper_inv = jnp.triu(diag_inv[step])
        solved, owner = solve_block(upper_inv, work, step)
        row_mask = global_rows < step * block_span
        work = apply_update(work, solved, owner, kept_columns[step], row_mask)
    return work


def solution(mesh):
    placed = (P("col", "row"), P("col", "row"), P())
    return jax.shard_map(
        body, mesh=mesh, in_specs=placed, out_specs=P("col", "row"), check_vma=False
    )
```

profile of v0, /device:TPU:0, one launch (start us, length us, event | category | flops | bytes accessed | tf_op | source)
XLA Modules:
  0.0 677.5 jit_solution(9635209791874704113)
XLA Ops:
  7.4 3.0 convolution_select_fusion.7
  10.3 0.0 all-reduce.9.cloned.1.call-update
  10.3 0.0 all-gather.2.cloned.1.call-start
  10.4 0.5 all-gather.2.cloned.1.call-update
  10.9 0.0 all-reduce.11.cloned.1.call-start
  11.0 74.3 %all-reduce.9.cloned.1.call-done = f32[512,128]{1,0:T(8,128)} async-done(((f32[512,128]{1,0:T(8,128)}), f32[512,128]{1,0:T(8,128)}) %all-reduce.9.cloned.1.call-update) | async-done | bytes 262160 | tf_op jit(solution)/shard_map/psum | solution.py:29
  85.3 35.6 %all-gather.2.cloned.1.call-done = bf16[4096,2048]{1,0:T(8,128)(2,1)} async-done(((bf16[4096,512]{1,0:T(8,128)(2,1)}), bf16[4096,2048]{1,0:T(8,128)(2,1)}) %all-gather.2.cloned.1.call-update) | async-done | bytes 16777232 | tf_op jit(solution)/shard_map/all_gather | solution.py:18
  120.9 3.6 fusion.15
  124.6 2.9 convolution_select_fusion.6
  127.5 0.0 all-reduce.11.cloned.1.call-update
  127.5 0.0 all-reduce.13.cloned.1.call-start
  127.6 1.3 slice.106
  129.0 69.8 %all-reduce.11.cloned.1.call-done = f32[512,128]{1,0:T(8,128)} async-done(((f32[512,128]{1,0:T(8,128)}), f32[512,128]{1,0:T(8,128)}) %all-reduce.11.cloned.1.call-update) | async-done | bytes 262160 | tf_op jit(solution)/shard_map/psum | solution.py:29
  198.8 4.1 fusion.13
  202.9 2.9 convolution_select_fusion.5
  205.8 0.0 all-reduce.13.cloned.1.call-update
  205.9 0.0 all-reduce.15.cloned.1.call-start
  205.9 1.3 slice.109
  207.3 68.9 %all-reduce.13.cloned.1.call-done = f32[512,128]{1,0:T(8,128)} async-done(((f32[512,128]{1,0:T(8,128)}), f32[512,128]{1,0:T(8,128)}) %all-reduce.13.cloned.1.call-update) | async-done | bytes 262160 | tf_op jit(solution)/shard_map/psum | solution.py:29
  276.2 4.1 fusion.11
  280.3 2.9 convolution_select_fusion.4
  283.3 0.0 all-reduce.15.cloned.1.call-update
  283.3 0.0 all-reduce.17.cloned.1.call-start
  283.4 1.3 slice.112
  284.7 69.0 %all-reduce.15.cloned.1.call-done = f32[512,128]{1,0:T(8,128)} async-done(((f32[512,128]{1,0:T(8,128)}), f32[512,128]{1,0:T(8,128)}) %all-reduce.15.cloned.1.call-update) | async-done | bytes 262160 | tf_op jit(solution)/shard_map/psum | solution.py:29
  353.7 4.2 fusion.9
  358.0 3.0 convolution_select_fusion.3
  361.0 0.0 all-reduce.19.cloned.1.call-start
  361.0 1.3 slice.115
  362.4 69.0 %all-reduce.17.cloned.1.call-done = f32[512,128]{1,0:T(8,128)} async-done(((f32[512,128]{1,0:T(8,128)}), f32[512,128]{1,0:T(8,128)}) %all-reduce.17.cloned.1.call-update) | async-done | bytes 262160 | tf_op jit(solution)/shard_map/psum | solution.py:29
  431.4 4.2 fusion.7
  435.6 3.0 convolution_select_fusion.2
  438.6 0.2 all-reduce.21.cloned.1.call-start
  438.9 1.3 slice.117
  440.2 68.8 %all-reduce.19.cloned.1.call-done = f32[512,128]{1,0:T(8,128)} async-done(((f32[512,128]{1,0:T(8,128)}), f32[512,128]{1,0:T(8,128)}) %all-reduce.19.cloned.1.call-update) | async-done | bytes 262160 | tf_op jit(solution)/shard_map/psum | solution.py:29
  509.0 4.1 fusion.5
  513.1 3.0 convolution_select_fusion.1
  516.1 0.0 all-reduce.23.cloned.1.call-start
  516.2 1.3 slice.119
  517.5 68.9 %all-reduce.21.cloned.1.call-done = f32[512,128]{1,0:T(8,128)} async-done(((f32[512,128]{1,0:T(8,128)}), f32[512,128]{1,0:T(8,128)}) %all-reduce.21.cloned.1.call-update) | async-done | bytes 262160 | tf_op jit(solution)/shard_map/psum | solution.py:29
  586.5 4.1 fusion.3
  590.6 3.0 convolution_select_fusion
  593.7 1.3 slice.121
  595.0 69.1 %all-reduce.23.cloned.1.call-done = f32[512,128]{1,0:T(8,128)} async-done(((f32[512,128]{1,0:T(8,128)}), f32[512,128]{1,0:T(8,128)}) %all-reduce.23.cloned.1.call-update) | async-done | bytes 262160 | tf_op jit(solution)/shard_map/psum | solution.py:29
  664.1 3.6 fusion.1
  667.6 0.1 slice.123
  667.8 0.8 copy-done.3
  668.6 1.5 pad_maximum_fusion
  (37 shorter events, 0.5 us)
Async XLA Ops:
  7.4 77.9 %all-reduce.9.cloned.1.call-start = ((), (), s32[]{:S(2)}) async-start(), calls=%async_computation | async-start | bytes 524288 | tf_op jit(solution)/shard_map/psum | solution.py:29
  10.3 110.6 %all-gather.2.cloned.1.call-start = ((), (), s32[]{:S(2)}) async-start(), calls=%async_computation.1 | async-start | bytes 20971520 | tf_op jit(solution)/shard_map/all_gather | solution.py:18
  10.9 187.8 %all-reduce.11.cloned.1.call-start = ((), (), s32[]{:S(2)}) async-start(), calls=%async_computation.2 | async-start | bytes 524288 | tf_op jit(solution)/shard_map/psum | solution.py:29
  85.3 39.3 %copy-start = (f32[512,128]{1,0:T(8,128)S(1)}, f32[512,128]{1,0:T(8,128)}, u32[]{:S(2)}) copy-start(f32[512,128]{1,0:T(8,128)} %all-reduce.9.cloned.1.call-done) | copy-start | bytes 786436
  127.5 148.7 %all-reduce.13.cloned.1.call-start = ((), (), s32[]{:S(2)}) async-start(), calls=%async_computation.3 | async-start | bytes 524288 | tf_op jit(solution)/shard_map/psum | solution.py:29
  198.7 4.1 copy-start.2
  205.9 147.8 %all-reduce.15.cloned.1.call-start = ((), (), s32[]{:S(2)}) async-start(), calls=%async_computation.4 | async-start | bytes 524288 | tf_op jit(solution)/shard_map/psum | solution.py:29
  276.2 4.1 copy-start.1
  283.3 148.1 %all-reduce.17.cloned.1.call-start = ((), (), s32[]{:S(2)}) async-start(), calls=%async_computation.5 | async-start | bytes 524288 | tf_op jit(solution)/shard_map/psum | solution.py:29
  353.7 4.2 copy-start.4
  361.0 148.0 %all-reduce.19.cloned.1.call-start = ((), (), s32[]{:S(2)}) async-start(), calls=%async_computation.6 | async-start | bytes 524288 | tf_op jit(solution)/shard_map/psum | solution.py:29
  431.4 4.2 copy-start.5
  438.6 147.8 %all-reduce.21.cloned.1.call-start = ((), (), s32[]{:S(2)}) async-start(), calls=%async_computation.7 | async-start | bytes 524288 | tf_op jit(solution)/shard_map/psum | solution.py:29
  509.0 4.1 copy-start.6
  516.1 147.9 %all-reduce.23.cloned.1.call-start = ((), (), s32[]{:S(2)}) async-start(), calls=%async_computation.8 | async-start | bytes 524288 | tf_op jit(solution)/shard_map/psum | solution.py:29
  586.5 4.1 copy-start.7
  667.6 1.0 copy-start.3
Sparse Core Ops, SparseCore 0:
  11.5 73.7 all-reduce.8
  127.7 71.0 all-reduce.10
  206.0 70.1 all-reduce.12
  283.4 70.2 all-reduce.14
  361.1 70.2 all-reduce.16
  438.8 70.1 all-reduce.18
  516.2 70.1 all-reduce.20
  593.8 70.2 all-reduce.22
Sparse Core Ops, SparseCore 1:
  12.4 108.5 all-gather.1
where the time goes:
time: 678 us
  waiting for transfers between devices  594 us (88%)
  matrix products  55.6 us (8%)
  between operations  15.2 us (2%)
  local copies, waits for them, and re-layouts  10.4 us (2%)
    psum x8, waiting for transfers between devices, solve_block(): solved = lax.psum(jnp.where(owner, product, jnp.float32(0.0)), 'col')  558 us
    all_gather x1, waiting for transfers between devices, body(): panel_rows = lax.all_gather(factors, 'row', axis=1, tiled=True)  35.6 us
    dot_general x8, matrix products, apply_update(): jnp.dot(columns, solved.astype(jnp.bfloat16), preferred_element_type=jnp....  32 us
    dot_general x8, matrix products, solve_block(): jnp.dot(matrix, work[:block], precision=lax.Precision.HIGHEST, preferred_...  23.6 us
  transfers between devices with their start and end apart: 9, of which 9 were waited for; matrix products, arithmetic and copies ran while one was open for 1% of the time, Pallas kernels for 0%

commit v1 on v0

v1 whole, which is shorter than its diff:
```python
import functools

import jax
import jax.numpy as jnp
from jax import lax
from jax.experimental import pallas as pl
from jax.experimental.pallas import tpu as pltpu
from jax.sharding import PartitionSpec as P

MESH = pl.DeviceIdType.MESH
F32 = jnp.float32
BF16 = jnp.bfloat16
CHUNKS = 8


def remote(src, dst, send_sem, recv_sem, **device):
    return pltpu.make_async_remote_copy(
        src_ref=src,
        dst_ref=dst,
        send_sem=send_sem,
        recv_sem=recv_sem,
        device_id=device,
        device_id_type=MESH,
    )


def dot(a, b):
    return jnp.dot(a, b, preferred_element_type=F32)


def split(value):
    high = value.astype(BF16)
    return high, (value - high.astype(F32)).astype(BF16)


def kernel(
    n_row, n_col, steps, block,
    rhs_ref, factors_ref, diag_ref, out_ref,
    diag, low_hi, low_lo, up_hi, up_lo, panel, solved, last, work, gathered,
    send1, recv1, own1, send2, recv2,
    diag_sem, f_send, f_recv, f_fwd, s_chain, s_side, s_row, s_recv, s_last, g_local, g_recv,
    one_send, one_recv, two_send, two_recv,
):
    rows_dev, width = rhs_ref.shape
    cols = factors_ref.shape[1]
    pieces = block // cols
    chips = n_row // 2
    side = n_col // steps
    row = lax.axis_index("row")
    col = lax.axis_index("col")
    chip, core = row // 2, row % 2
    sibling = chip * 2 + 1 - core
    zone, lane = col // side, col % side
    owner = lane == 0
    base = zone * side

    diag_copy = pltpu.make_async_copy(diag_ref.at[zone], diag, diag_sem)
    diag_copy.start()

    barrier = pltpu.get_barrier_semaphore()
    for d in range(1, n_row):
        pl.semaphore_signal(barrier, inc=1, device_id={"row": (row + d) % n_row}, device_id_type=MESH)
    for d in range(1, n_col):
        pl.semaphore_signal(barrier, inc=1, device_id={"col": (col + d) % n_col}, device_id_type=MESH)
    diag_copy.wait()
    pl.semaphore_wait(barrier, n_row + n_col - 2)

    window = factors_ref.at[pl.ds(0, block)]
    far = [((chip + d) % chips) * 2 + core for d in range(1, chips)]
    sends_panel = jnp.logical_and(owner, row // pieces != zone)

    def panel_copy(d):
        return remote(window, panel.at[row], f_send.at[d], f_recv.at[row], row=far[d - 1] if d else sibling)

    @pl.when(sends_panel)
    def _():
        for d in list(range(1, chips)) + [0]:
            panel_copy(d).start()

    @pl.when(owner)
    def _():
        down = lax.broadcasted_iota(jnp.int32, (block, block), 0)
        across = lax.broadcasted_iota(jnp.int32, (block, block), 1)
        matrix = diag[...]
        low_hi[...], low_lo[...] = split(jnp.where(down > across, matrix, 0.0))
        up_hi[...], up_lo[...] = split(jnp.where(down <= across, matrix, 0.0))
        work[...] = rhs_ref[pl.ds(0, block)]

    def solve(hi, lo):
        high, low = split(work[...])
        return dot(hi[...], high) + (dot(hi[...], low) + dot(lo[...], high))

    def forward_piece(source):
        return remote(panel.at[source], panel.at[source], f_fwd.at[source // 2], f_recv.at[source], row=sibling)

    def arrive_panel(j):
        for p in range(pieces):
            source = j * pieces + p

            @pl.when(source != row)
            def _():
                forward_piece(source).wait_recv()

            @pl.when(jnp.logical_and(source != row, source % 2 == core))
            def _():
                forward_piece(source).start()

            @pl.when(source == row)
            def _():
                panel[row] = factors_ref[pl.ds(0, block)]

    def chain_copy(t, j):
        target = jnp.where(t <= zone, zone + 1, zone - 1)
        return remote(solved.at[j], solved.at[j], s_chain.at[t], s_recv.at[j], col=target * side)

    def chain_sends(t):
        return jnp.where(t <= zone, zone < steps - 1, zone > 0)

    def side_copy(t, j, d):
        return remote(solved.at[j], solved.at[j], s_side.at[t, d], s_recv.at[j], col=base + d)

    def row_copy(t, j, p):
        dest = j * pieces + p
        part = solved.at[j, pl.ds(p * cols, cols)]
        return remote(
            part, gathered.at[core, :, pl.ds(pl.multiple_of(chip * width, width), width)],
            s_row.at[t, p], g_recv.at[row], row=dest,
        )

    def local_copy(j, p):
        part = solved.at[j, pl.ds(p * cols, cols)]
        return pltpu.make_async_copy(
            part, gathered.at[core, :, pl.ds(pl.multiple_of(chip * width, width), width)], g_local
        )

    for t in range(steps):
        j = jnp.where(t <= zone, t, steps + zone - t)
        mine = jnp.logical_and(owner, t == zone)

        @pl.when(jnp.logical_and(owner, t != zone))
        def _():
            arrive_panel(j)

        @pl.when(mine)
        def _():
            value = work[...] + solve(low_hi, low_lo)
            work[...] = value
            solved[j] = value.astype(BF16)

        @pl.when(jnp.logical_not(mine))
        def _():
            chain_copy(t, j).wait_recv()

        @pl.when(jnp.logical_and(owner, chain_sends(t)))
        def _():
            chain_copy(t, j).start()

        @pl.when(owner)
        def _():
            for d in range(1, side):
                side_copy(t, j, d).start()

        for p in range(pieces):
            @pl.when(j * pieces + p != row)
            def _():
                row_copy(t, j, p).start()

            @pl.when(j * pieces + p == row)
            def _():
                local_copy(j, p).start()

        @pl.when(jnp.logical_and(owner, t != zone))
        def _():
            total = work[...]
            for p in range(pieces):
                total = total - dot(panel[j * pieces + p], solved[j, pl.ds(p * cols, cols)])
            work[...] = total

    last_copy = remote(last, solved.at[zone], s_last, s_recv.at[zone], col=jnp.where(zone > 0, zone - 1, 0) * side)

    @pl.when(owner)
    def _():
        value = solve(up_hi, up_lo)
        work[...] = value
        last[...] = value.astype(BF16)

    @pl.when(jnp.logical_and(owner, zone > 0))
    def _():
        last_copy.start()

    local_copy(0, 0).wait()
    for d in range(1, n_row):
        source = (row + d) % n_row
        remote(
            gathered.at[source % 2, :, pl.ds(pl.multiple_of((source // 2) * width, width), width)],
            gathered.at[source % 2, :, pl.ds(pl.multiple_of((source // 2) * width, width), width)],
            g_local, g_recv.at[source], row=source,
        ).wait_recv()

    step_rows = rows_dev // CHUNKS

    def span(m):
        return pl.ds(pl.multiple_of(m * step_rows, step_rows), step_rows)

    def one_copy(m):
        return remote(send1.at[m], recv1.at[m], one_send.at[m], one_recv.at[m], row=sibling)

    def two_copy(m, d):
        return remote(send2.at[m, d - 1], recv2.at[m, d - 1], two_send.at[m, d - 1], two_recv.at[m, d - 1], row=far[d - 1])

    def first(m, carry):
        send1[m] = dot(factors_ref[span(m)], gathered[1 - core]).astype(BF16)
        one_copy(m).start()
        return carry

    def second(m, carry):
        own1[m] = dot(factors_ref[span(m)], gathered[core])
        one_copy(m).wait_recv()
        for d in range(1, chips):
            there = pl.ds(pl.multiple_of(((chip + d) % chips) * width, width), width)
            send2[m, d - 1] = (own1[m, :, there] + recv1[m, :, there].astype(F32)).astype(BF16)
            two_copy(m, d).start()
        return carry

    def third(m, carry):
        here = pl.ds(pl.multiple_of(chip * width, width), width)
        total = own1[m, :, here] + recv1[m, :, here].astype(F32)
        for d in range(1, chips):
            two_copy(m, d).wait_recv()
            total = total + recv2[m, d - 1].astype(F32)
        out_ref[span(m)] = rhs_ref[span(m)] - total
        return carry

    def finish(m, carry):
        one_copy(m).wait_send()
        for d in range(1, chips):
            two_copy(m, d).wait_send()
        return carry

    lax.fori_loop(0, CHUNKS, first, 0)
    lax.fori_loop(0, CHUNKS, second, 0)
    lax.fori_loop(0, CHUNKS, third, 0)

    @pl.when(owner)
    def _():
        out_ref[pl.ds(0, block)] = work[...]

    lax.fori_loop(0, CHUNKS, finish, 0)

    @pl.when(sends_panel)
    def _():
        for d in range(chips):
            panel_copy(d).wait_send()

    for t in range(steps):
        j = jnp.where(t <= zone, t, steps + zone - t)

        @pl.when(jnp.logical_and(owner, t != zone))
        def _():
            for p in range(pieces):
                source = j * pieces + p

                @pl.when(jnp.logical_and(source != row, source % 2 == core))
                def _():
                    forward_piece(source).wait_send()

        @pl.when(jnp.logical_and(owner, chain_sends(t)))
        def _():
            chain_copy(t, j).wait_send()

        @pl.when(owner)
        def _():
            for d in range(1, side):
                side_copy(t, j, d).wait_send()

        for p in range(pieces):
            @pl.when(j * pieces + p != row)
            def _():
                row_copy(t, j, p).wait_send()

    @pl.when(jnp.logical_and(owner, zone > 0))
    def _():
        last_copy.wait_send()


def body(rhs, factors, diag_inv):
    n_row, n_col = lax.axis_size("row"), lax.axis_size("col")
    rows_dev, width = rhs.shape
    cols = factors.shape[1]
    steps, block = diag_inv.shape[:2]
    pieces, chips, side = block // cols, n_row // 2, n_col // steps
    step_rows = rows_dev // CHUNKS
    dma = pltpu.SemaphoreType.DMA
    vmem = pl.BlockSpec(memory_space=pltpu.VMEM)
    return pl.pallas_call(
        functools.partial(kernel, n_row, n_col, steps, block),
        out_shape=jax.ShapeDtypeStruct(rhs.shape, F32),
        in_specs=[vmem, vmem, pl.BlockSpec(memory_space=pl.ANY)],
        out_specs=vmem,
        scratch_shapes=[
            pltpu.VMEM((block, block), F32),
            pltpu.VMEM((block, block), BF16),
            pltpu.VMEM((block, block), BF16),
            pltpu.VMEM((block, block), BF16),
            pltpu.VMEM((block, block), BF16),
            pltpu.VMEM((n_row, block, cols), BF16),
            pltpu.VMEM((steps, block, width), BF16),
            pltpu.VMEM((block, width), BF16),
            pltpu.VMEM((block, width), F32),
            pltpu.VMEM((2, cols, chips * width), BF16),
            pltpu.VMEM((CHUNKS, step_rows, chips * width), BF16),
            pltpu.VMEM((CHUNKS, step_rows, chips * width), BF16),
            pltpu.VMEM((CHUNKS, step_rows, chips * width), F32),
            pltpu.VMEM((CHUNKS, chips - 1, step_rows, width), BF16),
            pltpu.VMEM((CHUNKS, chips - 1, step_rows, width), BF16),
            dma, dma((chips,)), dma((n_row,)), dma((chips,)),
            dma((steps,)), dma((steps, side)), dma((steps, pieces)), dma((steps,)), dma, dma, dma((n_row,)),
            dma((CHUNKS,)), dma((CHUNKS,)), dma((CHUNKS, chips - 1)), dma((CHUNKS, chips - 1)),
        ],
        compiler_params=pltpu.CompilerParams(
            collective_id=0, has_side_effects=True, vmem_limit_bytes=60 * 1024 * 1024
        ),
    )(rhs, factors, diag_inv)


def solution(mesh):
    placed = (P("col", "row"), P("col", "row"), P())
    return jax.shard_map(
        body, mesh=mesh, in_specs=placed, out_specs=P("col", "row"), check_vma=False
    )
```

time: 678 us -> 89.3 us (0.13)
  the two profiles are of different devices: /device:TPU:0 before, /device:TPU:7 now
where the time goes in v1:
time: 89.3 us; the launch traced here: 89.2 us
  Pallas kernels  86.1 us (96%)
  local copies, waits for them, and re-layouts  3.05 us (3%)
    pallas_call x1, Pallas kernels, body(): pl.pallas_call(functools.partial(kernel, n_row, n_col, steps, block), out...  86.1 us
    unnamed x1, local copies, waits for them, and re-layouts  3.05 us

profile of v1, /device:TPU:7, one launch (start us, length us, event | category | flops | bytes accessed | tf_op | source)
XLA Modules:
  0.0 89.2 jit_solution(2138264395344726034)
XLA Ops:
  0.0 86.1 %shard_map.37 = f32[4096,128]{1,0:T(8,128)} custom-call(f32[4096,128]{1,0:T(8,128)} %rhs_ref.1, bf16[4096,512]{1,0:T(8,128)(2,1)} %factors_ref.1, f32[4,512,512]{2,1,0:T(8,128)} %diag_ref.1), custom_call_target="tpu_custom_call" | custom-call | tf_op jit(solution)/shard_map/pallas_call | solution.py:295
  86.1 3.0 %copy.5 = f32[4096,128]{1,0:T(8,128)} copy(f32[4096,128]{1,0:T(8,128)} %shard_map.37) | data formatting | bytes 4194304

commit v2 on v1

--- a/solution.py
+++ b/solution.py
@@ -11,6 +11,7 @@
 F32 = jnp.float32
 BF16 = jnp.bfloat16
 CHUNKS = 8
+PARTS = 4
 
 
 def remote(src, dst, send_sem, recv_sem, **device):
@@ -86,9 +87,13 @@
         up_hi[...], up_lo[...] = split(jnp.where(down <= across, matrix, 0.0))
         work[...] = rhs_ref[pl.ds(0, block)]
 
-    def solve(hi, lo):
-        high, low = split(work[...])
-        return dot(hi[...], high) + (dot(hi[...], low) + dot(lo[...], high))
+    part_rows = block // PARTS
+
+    def part(q):
+        return pl.ds(q * part_rows, part_rows)
+
+    def solve(hi, lo, high, low, q):
+        return dot(hi[part(q)], high) + (dot(hi[part(q)], low) + dot(lo[part(q)], high))
 
     def forward_piece(source):
         return remote(panel.at[source], panel.at[source], f_fwd.at[source // 2], f_recv.at[source], row=sibling)
@@ -109,15 +114,38 @@
             def _():
                 panel[row] = factors_ref[pl.ds(0, block)]
 
-    def chain_copy(t, j):
+    def chain_copy(t, j, q):
         target = jnp.where(t <= zone, zone + 1, zone - 1)
-        return remote(solved.at[j], solved.at[j], s_chain.at[t], s_recv.at[j], col=target * side)
+        piece = solved.at[j, part(q)]
+        return remote(piece, piece, s_chain.at[t, q], s_recv.at[j, q], col=target * side)
 
     def chain_sends(t):
         return jnp.where(t <= zone, zone < steps - 1, zone > 0)
 
-    def side_copy(t, j, d):
-        return remote(solved.at[j], solved.at[j], s_side.at[t, d], s_recv.at[j], col=base + d)
+    def side_copy(t, j, d, q):
+        piece = solved.at[j, part(q)]
+        return remote(piece, piece, s_side.at[t, d, q], s_recv.at[j, q], col=base + d)
+
+    def pass_on(t, j, q):
+        @pl.when(jnp.logical_and(owner, chain_sends(t)))
+        def _():
+            chain_copy(t, j, q).start()
+
+        @pl.when(owner)
+        def _():
+            for d in range(1, side):
+                side_copy(t, j, d, q).start()
+
+    def update(j, q):
+        first_row = (q - 1) * part_rows
+        total = work[...]
+        depth = min(2 * part_rows, cols)
+        for start in range(first_row, first_row + 2 * part_rows, depth):
+            total = total - dot(
+                panel[j * pieces + start // cols, :, pl.ds(start % cols, depth)],
+                solved[j, pl.ds(start, depth)],
+            )
+        work[...] = total
 
     def row_copy(t, j, p):
         dest = j * pieces + p
@@ -132,70 +160,6 @@
         return pltpu.make_async_copy(
             part, gathered.at[core, :, pl.ds(pl.multiple_of(chip * width, width), width)], g_local
         )
-
-    for t in range(steps):
-        j = jnp.where(t <= zone, t, steps + zone - t)
-        mine = jnp.logical_and(owner, t == zone)
-
-        @pl.when(jnp.logical_and(owner, t != zone))
-        def _():
-            arrive_panel(j)
-
-        @pl.when(mine)
-        def _():
-            value = work[...] + solve(low_hi, low_lo)
-            work[...] = value
-            solved[j] = value.astype(BF16)
-
-        @pl.when(jnp.logical_not(mine))
-        def _():
-            chain_copy(t, j).wait_recv()
-
-        @pl.when(jnp.logical_and(owner, chain_sends(t)))
-        def _():
-            chain_copy(t, j).start()
-
-        @pl.when(owner)
-        def _():
-            for d in range(1, side):
-                side_copy(t, j, d).start()
-
-        for p in range(pieces):
-            @pl.when(j * pieces + p != row)
-            def _():
-                row_copy(t, j, p).start()
-
-            @pl.when(j * pieces + p == row)
-            def _():
-                local_copy(j, p).start()
-
-        @pl.when(jnp.logical_and(owner, t != zone))
-        def _():
-            total = work[...]
-            for p in range(pieces):
-                total = total - dot(panel[j * pieces + p], solved[j, pl.ds(p * cols, cols)])
-            work[...] = total
-
-    last_copy = remote(last, solved.at[zone], s_last, s_recv.at[zone], col=jnp.where(zone > 0, zone - 1, 0) * side)
-
-    @pl.when(owner)
-    def _():
-        value = solve(up_hi, up_lo)
-        work[...] = value
-        last[...] = value.astype(BF16)
-
-    @pl.when(jnp.logical_and(owner, zone > 0))
-    def _():
-        last_copy.start()
-
-    local_copy(0, 0).wait()
-    for d in range(1, n_row):
-        source = (row + d) % n_row
-        remote(
-            gathered.at[source % 2, :, pl.ds(pl.multiple_of((source // 2) * width, width), width)],
-            gathered.at[source % 2, :, pl.ds(pl.multiple_of((source // 2) * width, width), width)],
-            g_local, g_recv.at[source], row=source,
-        ).wait_recv()
 
     step_rows = rows_dev // CHUNKS
 
@@ -237,7 +201,73 @@
             two_copy(m, d).wait_send()
         return carry
 
-    lax.fori_loop(0, CHUNKS, first, 0)
+    mine_block = row // pieces
+    place = jnp.where(mine_block <= zone, mine_block, steps + zone - mine_block)
+    early = jnp.logical_and(place < steps - 1, lane > 0)
+
+    def first_products():
+        local_copy(0, 0).wait()
+        for d in range(1, n_row):
+            source = (row + d) % n_row
+            piece = gathered.at[source % 2, :, pl.ds(pl.multiple_of((source // 2) * width, width), width)]
+            remote(piece, piece, g_local, g_recv.at[source], row=source).wait_recv()
+        lax.fori_loop(0, CHUNKS, first, 0)
+
+    for t in range(steps):
+        j = jnp.where(t <= zone, t, steps + zone - t)
+        mine = jnp.logical_and(owner, t == zone)
+        if t == steps - 1:
+            pl.when(early)(first_products)
+
+        @pl.when(jnp.logical_and(owner, t != zone))
+        def _():
+            arrive_panel(j)
+
+        @pl.when(mine)
+        def _():
+            high, low = split(work[...])
+            for q in range(PARTS):
+                value = work[part(q)] + solve(low_hi, low_lo, high, low, q)
+                work[part(q)] = value
+                solved[j, part(q)] = value.astype(BF16)
+                pass_on(t, j, q)
+
+        @pl.when(jnp.logical_not(mine))
+        def _():
+            for q in range(PARTS):
+                chain_copy(t, j, q).wait_recv()
+                pass_on(t, j, q)
+                if q % 2:
+                    @pl.when(owner)
+                    def _():
+                        update(j, q)
+
+        for p in range(pieces):
+            @pl.when(j * pieces + p != row)
+            def _():
+                row_copy(t, j, p).start()
+
+            @pl.when(j * pieces + p == row)
+            def _():
+                local_copy(j, p).start()
+
+    def last_copy(q):
+        target = jnp.where(zone > 0, zone - 1, 0) * side
+        return remote(last.at[part(q)], solved.at[zone, part(q)], s_last.at[q], s_recv.at[zone, q], col=target)
+
+    @pl.when(owner)
+    def _():
+        high, low = split(work[...])
+        for q in range(PARTS):
+            value = solve(up_hi, up_lo, high, low, q)
+            work[part(q)] = value
+            last[part(q)] = value.astype(BF16)
+
+            @pl.when(zone > 0)
+            def _():
+                last_copy(q).start()
+
+    pl.when(jnp.logical_not(early))(first_products)
     lax.fori_loop(0, CHUNKS, second, 0)
     lax.fori_loop(0, CHUNKS, third, 0)
 
@@ -266,12 +296,14 @@
 
         @pl.when(jnp.logical_and(owner, chain_sends(t)))
         def _():
-            chain_copy(t, j).wait_send()
+            for q in range(PARTS):
+                chain_copy(t, j, q).wait_send()
 
         @pl.when(owner)
         def _():
             for d in range(1, side):
-                side_copy(t, j, d).wait_send()
+                for q in range(PARTS):
+                    side_copy(t, j, d, q).wait_send()
 
         for p in range(pieces):
             @pl.when(j * pieces + p != row)
@@ -280,7 +312,8 @@
 
     @pl.when(jnp.logical_and(owner, zone > 0))
     def _():
-        last_copy.wait_send()
+        for q in range(PARTS):
+            last_copy(q).wait_send()
 
 
 def body(rhs, factors, diag_inv):
@@ -314,7 +347,7 @@
             pltpu.VMEM((CHUNKS, chips - 1, step_rows, width), BF16),
             pltpu.VMEM((CHUNKS, chips - 1, step_rows, width), BF16),
             dma, dma((chips,)), dma((n_row,)), dma((chips,)),
-            dma((steps,)), dma((steps, side)), dma((steps, pieces)), dma((steps,)), dma, dma, dma((n_row,)),
+            dma((steps, PARTS)), dma((steps, side, PARTS)), dma((steps, pieces)), dma((steps, PARTS)), dma((PARTS,)), dma, dma((n_row,)),
             dma((CHUNKS,)), dma((CHUNKS,)), dma((CHUNKS, chips - 1)), dma((CHUNKS, chips - 1)),
         ],
         compiler_params=pltpu.CompilerParams(

time: 89.3 us -> 86.3 us (0.966)
  Pallas kernels: 86.1 us -> 83 us
    pallas_call x1, Pallas kernels: 86.1 us -> 83 us  [body(): pl.pallas_call(functools.partial(kernel, n_row, n_col, steps, block), out...]
where the time goes in v2:
time: 86.3 us; the launch traced here: 86.1 us
  Pallas kernels  83 us (96%)
  local copies, waits for them, and re-layouts  3.05 us (4%)
    pallas_call x1, Pallas kernels, body(): pl.pallas_call(functools.partial(kernel, n_row, n_col, steps, block), out...  83 us
    unnamed x1, local copies, waits for them, and re-layouts  3.05 us

profile of v2, /device:TPU:7, one launch (start us, length us, event | category | flops | bytes accessed | tf_op | source)
XLA Modules:
  0.0 86.1 jit_solution(17629354264353267428)
XLA Ops:
  0.0 83.0 %shard_map.37 = f32[4096,128]{1,0:T(8,128)} custom-call(f32[4096,128]{1,0:T(8,128)} %rhs_ref.1, bf16[4096,512]{1,0:T(8,128)(2,1)} %factors_ref.1, f32[4,512,512]{2,1,0:T(8,128)} %diag_ref.1), custom_call_target="tpu_custom_call" | custom-call | tf_op jit(solution)/shard_map/pallas_call | solution.py:328
  83.0 3.0 %copy.5 = f32[4096,128]{1,0:T(8,128)} copy(f32[4096,128]{1,0:T(8,128)} %shard_map.37) | data formatting | bytes 4194304

commit v3 on v2

--- a/solution.py
+++ b/solution.py
@@ -12,6 +12,7 @@
 BF16 = jnp.bfloat16
 CHUNKS = 8
 PARTS = 4
+GATHER = 3
 
 
 def remote(src, dst, send_sem, recv_sem, **device):
@@ -36,11 +37,12 @@
 
 def kernel(
     n_row, n_col, steps, block,
-    rhs_ref, factors_ref, diag_ref, out_ref,
+    rhs_hbm, factors_hbm, diag_ref, out_ref,
+    rhs_ref, factors_ref, extra,
     diag, low_hi, low_lo, up_hi, up_lo, panel, solved, last, work, gathered,
     send1, recv1, own1, send2, recv2,
     diag_sem, f_send, f_recv, f_fwd, s_chain, s_side, s_row, s_recv, s_last, g_local, g_recv,
-    one_send, one_recv, two_send, two_recv,
+    one_send, one_recv, two_send, two_recv, x_send, x_recv, x_fwd, load_sem,
 ):
     rows_dev, width = rhs_ref.shape
     cols = factors_ref.shape[1]
@@ -56,17 +58,24 @@
     base = zone * side
 
     diag_copy = pltpu.make_async_copy(diag_ref.at[zone], diag, diag_sem)
+    rhs_copy = pltpu.make_async_copy(rhs_hbm, rhs_ref, load_sem.at[0])
+    factors_copy = pltpu.make_async_copy(factors_hbm, factors_ref, load_sem.at[1])
+    work_copy = pltpu.make_async_copy(rhs_hbm.at[pl.ds(0, block)], work, load_sem.at[2])
+    panel_own = pltpu.make_async_copy(factors_hbm.at[pl.ds(0, block)], panel.at[row], load_sem.at[3])
     diag_copy.start()
+    work_copy.start()
+    panel_own.start()
+    factors_copy.start()
+    rhs_copy.start()
 
     barrier = pltpu.get_barrier_semaphore()
     for d in range(1, n_row):
         pl.semaphore_signal(barrier, inc=1, device_id={"row": (row + d) % n_row}, device_id_type=MESH)
     for d in range(1, n_col):
         pl.semaphore_signal(barrier, inc=1, device_id={"col": (col + d) % n_col}, device_id_type=MESH)
-    diag_copy.wait()
     pl.semaphore_wait(barrier, n_row + n_col - 2)
 
-    window = factors_ref.at[pl.ds(0, block)]
+    window = factors_hbm.at[pl.ds(0, block)]
     far = [((chip + d) % chips) * 2 + core for d in range(1, chips)]
     sends_panel = jnp.logical_and(owner, row // pieces != zone)
 
@@ -77,6 +86,31 @@
     def _():
         for d in list(range(1, chips)) + [0]:
             panel_copy(d).start()
+
+    step_rows = rows_dev // CHUNKS
+    n_extra = jnp.maximum(GATHER - zone - jnp.where(owner, 1, 0), 0)
+
+    def span(m):
+        return pl.ds(pl.multiple_of(m * step_rows, step_rows), step_rows)
+
+    def extra_copy(g, d):
+        return remote(
+            factors_hbm.at[span(CHUNKS - 1 - g)], extra.at[g, row], x_send.at[g, d], x_recv.at[g, row],
+            row=far[d - 1] if d else sibling,
+        )
+
+    def extra_forward(g, source):
+        return remote(extra.at[g, source], extra.at[g, source], x_fwd.at[g, source // 2], x_recv.at[g, source], row=sibling)
+
+    def extra_start(g, carry):
+        for d in range(chips):
+            extra_copy(g, d).start()
+        return carry
+
+    lax.fori_loop(0, n_extra, extra_start, 0)
+    diag_copy.wait()
+    work_copy.wait()
+    panel_own.wait()
 
     @pl.when(owner)
     def _():
@@ -85,7 +119,6 @@
         matrix = diag[...]
         low_hi[...], low_lo[...] = split(jnp.where(down > across, matrix, 0.0))
         up_hi[...], up_lo[...] = split(jnp.where(down <= across, matrix, 0.0))
-        work[...] = rhs_ref[pl.ds(0, block)]
 
     part_rows = block // PARTS
 
@@ -97,22 +130,29 @@
 
     def forward_piece(source):
         return remote(panel.at[source], panel.at[source], f_fwd.at[source // 2], f_recv.at[source], row=sibling)
+
+    def slot(t):
+        return jnp.where(t <= zone, t, steps + zone - t)
+
+    def hand_on(t):
+        if t == steps:
+            return
+        for p in range(pieces):
+            source = slot(t) * pieces + p
+            here = jnp.logical_and(owner, t != zone)
+
+            @pl.when(here & (source != row) & (source % 2 == core))
+            def _():
+                forward_piece(source).wait_recv()
+                forward_piece(source).start()
 
     def arrive_panel(j):
         for p in range(pieces):
             source = j * pieces + p
 
-            @pl.when(source != row)
+            @pl.when(source % 2 != core)
             def _():
                 forward_piece(source).wait_recv()
-
-            @pl.when(jnp.logical_and(source != row, source % 2 == core))
-            def _():
-                forward_piece(source).start()
-
-            @pl.when(source == row)
-            def _():
-                panel[row] = factors_ref[pl.ds(0, block)]
 
     def chain_copy(t, j, q):
         target = jnp.where(t <= zone, zone + 1, zone - 1)
@@ -161,11 +201,6 @@
             part, gathered.at[core, :, pl.ds(pl.multiple_of(chip * width, width), width)], g_local
         )
 
-    step_rows = rows_dev // CHUNKS
-
-    def span(m):
-        return pl.ds(pl.multiple_of(m * step_rows, step_rows), step_rows)
-
     def one_copy(m):
         return remote(send1.at[m], recv1.at[m], one_send.at[m], one_recv.at[m], row=sibling)
 
@@ -201,23 +236,53 @@
             two_copy(m, d).wait_send()
         return carry
 
-    mine_block = row // pieces
-    place = jnp.where(mine_block <= zone, mine_block, steps + zone - mine_block)
-    early = jnp.logical_and(place < steps - 1, lane > 0)
+    n_swap = CHUNKS - n_extra
+
+    def extra_hand_on(g, carry):
+        for d in range(1, chips):
+            extra_forward(g, far[d - 1]).wait_recv()
+            extra_forward(g, far[d - 1]).start()
+        return carry
+
+    def extra_product(g, carry):
+        rows = span(CHUNKS - 1 - g)
+        total = rhs_ref[rows]
+        for d in range(n_row):
+            source = (row + d) % n_row
+            part_of = solved[source // pieces, pl.ds(pl.multiple_of((source % pieces) * cols, cols), cols)]
+            if d == 0:
+                total = total - dot(factors_ref[rows], part_of)
+            else:
+                @pl.when(source % 2 != core)
+                def _():
+                    extra_forward(g, source).wait_recv()
+
+                total = total - dot(extra[g, source], part_of)
+        out_ref[rows] = total
+        return carry
+
+    def extra_finish(g, carry):
+        for d in range(chips):
+            extra_copy(g, d).wait_send()
+        for d in range(1, chips):
+            extra_forward(g, far[d - 1]).wait_send()
+        return carry
 
     def first_products():
+        factors_copy.wait()
+        rhs_copy.wait()
         local_copy(0, 0).wait()
         for d in range(1, n_row):
             source = (row + d) % n_row
             piece = gathered.at[source % 2, :, pl.ds(pl.multiple_of((source // 2) * width, width), width)]
             remote(piece, piece, g_local, g_recv.at[source], row=source).wait_recv()
-        lax.fori_loop(0, CHUNKS, first, 0)
+        lax.fori_loop(0, n_swap, first, 0)
 
     for t in range(steps):
-        j = jnp.where(t <= zone, t, steps + zone - t)
+        j = slot(t)
         mine = jnp.logical_and(owner, t == zone)
-        if t == steps - 1:
-            pl.when(early)(first_products)
+        if t == 0:
+            hand_on(t)
 
         @pl.when(jnp.logical_and(owner, t != zone))
         def _():
@@ -251,6 +316,8 @@
             def _():
                 local_copy(j, p).start()
 
+        hand_on(t + 1)
+
     def last_copy(q):
         target = jnp.where(zone > 0, zone - 1, 0) * side
         return remote(last.at[part(q)], solved.at[zone, part(q)], s_last.at[q], s_recv.at[zone, q], col=target)
@@ -267,15 +334,18 @@
             def _():
                 last_copy(q).start()
 
-    pl.when(jnp.logical_not(early))(first_products)
-    lax.fori_loop(0, CHUNKS, second, 0)
-    lax.fori_loop(0, CHUNKS, third, 0)
+    first_products()
+    lax.fori_loop(0, n_swap, second, 0)
+    lax.fori_loop(0, n_extra, extra_hand_on, 0)
+    lax.fori_loop(0, n_extra, extra_product, 0)
+    lax.fori_loop(0, n_swap, third, 0)
 
     @pl.when(owner)
     def _():
         out_ref[pl.ds(0, block)] = work[...]
 
-    lax.fori_loop(0, CHUNKS, finish, 0)
+    lax.fori_loop(0, n_swap, finish, 0)
+    lax.fori_loop(0, n_extra, extra_finish, 0)
 
     @pl.when(sends_panel)
     def _():
@@ -283,7 +353,7 @@
             panel_copy(d).wait_send()
 
     for t in range(steps):
-        j = jnp.where(t <= zone, t, steps + zone - t)
+        j = slot(t)
 
         @pl.when(jnp.logical_and(owner, t != zone))
         def _():
@@ -328,9 +398,12 @@
     return pl.pallas_call(
         functools.partial(kernel, n_row, n_col, steps, block),
         out_shape=jax.ShapeDtypeStruct(rhs.shape, F32),
-        in_specs=[vmem, vmem, pl.BlockSpec(memory_space=pl.ANY)],
+        in_specs=[pl.BlockSpec(memory_space=pl.ANY)] * 3,
         out_specs=vmem,
         scratch_shapes=[
+            pltpu.VMEM(rhs.shape, F32),
+            pltpu.VMEM(factors.shape, BF16),
+            pltpu.VMEM((GATHER, n_row, step_rows, cols), BF16),
             pltpu.VMEM((block, block), F32),
             pltpu.VMEM((block, block), BF16),
             pltpu.VMEM((block, block), BF16),
@@ -349,6 +422,7 @@
             dma, dma((chips,)), dma((n_row,)), dma((chips,)),
             dma((steps, PARTS)), dma((steps, side, PARTS)), dma((steps, pieces)), dma((steps, PARTS)), dma((PARTS,)), dma, dma((n_row,)),
             dma((CHUNKS,)), dma((CHUNKS,)), dma((CHUNKS, chips - 1)), dma((CHUNKS, chips - 1)),
+            dma((GATHER, chips)), dma((GATHER, n_row)), dma((GATHER, chips)), dma((4,)),
         ],
         compiler_params=pltpu.CompilerParams(
             collective_id=0, has_side_effects=True, vmem_limit_bytes=60 * 1024 * 1024

time: 86.3 us -> 77 us (0.89)
  the two profiles are of different devices: /device:TPU:7 before, /device:TPU:0 now
where the time goes in v3:
time: 77 us; the launch traced here: 76.9 us
  Pallas kernels  73.8 us (96%)
  local copies, waits for them, and re-layouts  3.05 us (4%)
    pallas_call x1, Pallas kernels, body(): pl.pallas_call(functools.partial(kernel, n_row, n_col, steps, block), out...  73.8 us
    unnamed x1, local copies, waits for them, and re-layouts  3.05 us

profile of v3, /device:TPU:0, one launch (start us, length us, event | category | flops | bytes accessed | tf_op | source)
XLA Modules:
  0.0 76.9 jit_solution(9598518871436753499)
XLA Ops:
  0.0 73.8 %shard_map.37 = f32[4096,128]{1,0:T(8,128)} custom-call(f32[4096,128]{1,0:T(8,128)} %rhs_hbm.1, bf16[4096,512]{1,0:T(8,128)(2,1)} %factors_hbm.1, f32[4,512,512]{2,1,0:T(8,128)} %diag_ref.1), custom_call_target="tpu_custom_call" | custom-call | tf_op jit(solution)/shard_map/pallas_call | solution.py:398
  73.8 3.0 %copy.5 = f32[4096,128]{1,0:T(8,128)} copy(f32[4096,128]{1,0:T(8,128)} %shard_map.37) | data formatting | bytes 4194304

commit v4 on v3

--- a/solution.py
+++ b/solution.py
@@ -44,7 +44,7 @@
     diag_sem, f_send, f_recv, f_fwd, s_chain, s_side, s_row, s_recv, s_last, g_local, g_recv,
     one_send, one_recv, two_send, two_recv, x_send, x_recv, x_fwd, load_sem,
 ):
-    rows_dev, width = rhs_ref.shape
+    rows_dev, width = rhs_hbm.shape
     cols = factors_ref.shape[1]
     pieces = block // cols
     chips = n_row // 2
@@ -58,7 +58,7 @@
     base = zone * side
 
     diag_copy = pltpu.make_async_copy(diag_ref.at[zone], diag, diag_sem)
-    rhs_copy = pltpu.make_async_copy(rhs_hbm, rhs_ref, load_sem.at[0])
+    rhs_copy = pltpu.make_async_copy(rhs_hbm.at[pl.ds(0, block)], rhs_ref, load_sem.at[0])
     factors_copy = pltpu.make_async_copy(factors_hbm, factors_ref, load_sem.at[1])
     work_copy = pltpu.make_async_copy(rhs_hbm.at[pl.ds(0, block)], work, load_sem.at[2])
     panel_own = pltpu.make_async_copy(factors_hbm.at[pl.ds(0, block)], panel.at[row], load_sem.at[3])
@@ -88,7 +88,7 @@
             panel_copy(d).start()
 
     step_rows = rows_dev // CHUNKS
-    n_extra = jnp.maximum(GATHER - zone - jnp.where(owner, 1, 0), 0)
+    n_extra = jnp.maximum(GATHER - (zone + 1) // 2 - jnp.where(owner, 1, 0), 0)
 
     def span(m):
         return pl.ds(pl.multiple_of(m * step_rows, step_rows), step_rows)
@@ -187,19 +187,28 @@
             )
         work[...] = total
 
-    def row_copy(t, j, p):
-        dest = j * pieces + p
-        part = solved.at[j, pl.ds(p * cols, cols)]
+    per = PARTS // pieces
+    my_columns = pl.ds(pl.multiple_of(chip * width, width), width)
+
+    def row_copy(t, j, q):
         return remote(
-            part, gathered.at[core, :, pl.ds(pl.multiple_of(chip * width, width), width)],
-            s_row.at[t, p], g_recv.at[row], row=dest,
+            solved.at[j, part(q)], gathered.at[core, part(q % per), my_columns],
+            s_row.at[t, q], g_recv.at[row, q % per], row=j * pieces + q // per,
         )
 
-    def local_copy(j, p):
-        part = solved.at[j, pl.ds(p * cols, cols)]
+    def local_copy(j, q):
         return pltpu.make_async_copy(
-            part, gathered.at[core, :, pl.ds(pl.multiple_of(chip * width, width), width)], g_local
+            solved.at[j, part(q)], gathered.at[core, part(q % per), my_columns], g_local.at[q % per]
         )
+
+    def share(t, j, q):
+        @pl.when(j * pieces + q // per != row)
+        def _():
+            row_copy(t, j, q).start()
+
+        @pl.when(j * pieces + q // per == row)
+        def _():
+            local_copy(j, q).start()
 
     def one_copy(m):
         return remote(send1.at[m], recv1.at[m], one_send.at[m], one_recv.at[m], row=sibling)
@@ -213,6 +222,10 @@
         return carry
 
     def second(m, carry):
+        @pl.when(m + 2 < n_swap)
+        def _():
+            first(m + 2, 0)
+
         own1[m] = dot(factors_ref[span(m)], gathered[core])
         one_copy(m).wait_recv()
         for d in range(1, chips):
@@ -227,7 +240,7 @@
         for d in range(1, chips):
             two_copy(m, d).wait_recv()
             total = total + recv2[m, d - 1].astype(F32)
-        out_ref[span(m)] = rhs_ref[span(m)] - total
+        out_ref[span(m)] = total
         return carry
 
     def finish(m, carry):
@@ -246,18 +259,18 @@
 
     def extra_product(g, carry):
         rows = span(CHUNKS - 1 - g)
-        total = rhs_ref[rows]
+        total = jnp.zeros((step_rows, width), F32)
         for d in range(n_row):
             source = (row + d) % n_row
             part_of = solved[source // pieces, pl.ds(pl.multiple_of((source % pieces) * cols, cols), cols)]
             if d == 0:
-                total = total - dot(factors_ref[rows], part_of)
+                total = total + dot(factors_ref[rows], part_of)
             else:
                 @pl.when(source % 2 != core)
                 def _():
                     extra_forward(g, source).wait_recv()
 
-                total = total - dot(extra[g, source], part_of)
+                total = total + dot(extra[g, source], part_of)
         out_ref[rows] = total
         return carry
 
@@ -271,12 +284,15 @@
     def first_products():
         factors_copy.wait()
         rhs_copy.wait()
-        local_copy(0, 0).wait()
+        for q in range(per):
+            local_copy(0, q).wait()
         for d in range(1, n_row):
             source = (row + d) % n_row
-            piece = gathered.at[source % 2, :, pl.ds(pl.multiple_of((source // 2) * width, width), width)]
-            remote(piece, piece, g_local, g_recv.at[source], row=source).wait_recv()
-        lax.fori_loop(0, n_swap, first, 0)
+            for q in range(per):
+                piece = gathered.at[source % 2, part(q), pl.ds(pl.multiple_of((source // 2) * width, width), width)]
+                remote(piece, piece, g_local.at[q], g_recv.at[source, q], row=source).wait_recv()
+        first(0, 0)
+        first(1, 0)
 
     for t in range(steps):
         j = slot(t)
@@ -296,25 +312,18 @@
                 work[part(q)] = value
                 solved[j, part(q)] = value.astype(BF16)
                 pass_on(t, j, q)
+                share(t, j, q)
 
         @pl.when(jnp.logical_not(mine))
         def _():
             for q in range(PARTS):
                 chain_copy(t, j, q).wait_recv()
                 pass_on(t, j, q)
+                share(t, j, q)
                 if q % 2:
                     @pl.when(owner)
                     def _():
                         update(j, q)
-
-        for p in range(pieces):
-            @pl.when(j * pieces + p != row)
-            def _():
-                row_copy(t, j, p).start()
-
-            @pl.when(j * pieces + p == row)
-            def _():
-                local_copy(j, p).start()
 
         hand_on(t + 1)
 
@@ -342,7 +351,7 @@
 
     @pl.when(owner)
     def _():
-        out_ref[pl.ds(0, block)] = work[...]
+        out_ref[pl.ds(0, block)] = rhs_ref[...] - work[...]
 
     lax.fori_loop(0, n_swap, finish, 0)
     lax.fori_loop(0, n_extra, extra_finish, 0)
@@ -375,10 +384,10 @@
                 for q in range(PARTS):
                     side_copy(t, j, d, q).wait_send()
 
-        for p in range(pieces):
-            @pl.when(j * pieces + p != row)
+        for q in range(PARTS):
+            @pl.when(j * pieces + q // per != row)
             def _():
-                row_copy(t, j, p).wait_send()
+                row_copy(t, j, q).wait_send()
 
     @pl.when(jnp.logical_and(owner, zone > 0))
     def _():
@@ -395,13 +404,13 @@
     step_rows = rows_dev // CHUNKS
     dma = pltpu.SemaphoreType.DMA
     vmem = pl.BlockSpec(memory_space=pltpu.VMEM)
-    return pl.pallas_call(
+    taken = pl.pallas_call(
         functools.partial(kernel, n_row, n_col, steps, block),
         out_shape=jax.ShapeDtypeStruct(rhs.shape, F32),
         in_specs=[pl.BlockSpec(memory_space=pl.ANY)] * 3,
         out_specs=vmem,
         scratch_shapes=[
-            pltpu.VMEM(rhs.shape, F32),
+            pltpu.VMEM((block, width), F32),
             pltpu.VMEM(factors.shape, BF16),
             pltpu.VMEM((GATHER, n_row, step_rows, cols), BF16),
             pltpu.VMEM((block, block), F32),
@@ -420,7 +429,8 @@
             pltpu.VMEM((CHUNKS, chips - 1, step_rows, width), BF16),
             pltpu.VMEM((CHUNKS, chips - 1, step_rows, width), BF16),
             dma, dma((chips,)), dma((n_row,)), dma((chips,)),
-            dma((steps, PARTS)), dma((steps, side, PARTS)), dma((steps, pieces)), dma((steps, PARTS)), dma((PARTS,)), dma, dma((n_row,)),
+            dma((steps, PARTS)), dma((steps, side, PARTS)), dma((steps, PARTS)), dma((steps, PARTS)), dma((PARTS,)),
+            dma((PARTS // pieces,)), dma((n_row, PARTS // pieces)),
             dma((CHUNKS,)), dma((CHUNKS,)), dma((CHUNKS, chips - 1)), dma((CHUNKS, chips - 1)),
             dma((GATHER, chips)), dma((GATHER, n_row)), dma((GATHER, chips)), dma((4,)),
         ],
@@ -428,6 +438,7 @@
             collective_id=0, has_side_effects=True, vmem_limit_bytes=60 * 1024 * 1024
         ),
     )(rhs, factors, diag_inv)
+    return rhs - taken
 
 
 def solution(mesh):

time: 77 us -> 77.2 us (level)
  other arithmetic: 0 us -> 3.12 us
  local copies, waits for them, and re-layouts: 3.05 us -> 0.01 us
    sub x0 -> x1, other arithmetic: none -> 3.12 us  [body(): return rhs - taken]
    unnamed x1 -> x2, local copies, waits for them, and re-layouts: 3.05 us -> 0.01 us
where the time goes in v4:
time: 77.2 us; the launch traced here: 77 us
  Pallas kernels  73.9 us (96%)
  other arithmetic  3.12 us (4%)
    pallas_call x1, Pallas kernels, body(): pl.pallas_call(functools.partial(kernel, n_row, n_col, steps, block), out...  73.9 us
    sub x1, other arithmetic, body(): return rhs - taken  3.12 us

profile of v4, /device:TPU:0, one launch (start us, length us, event | category | flops | bytes accessed | tf_op | source)
XLA Modules:
  0.0 77.0 jit_solution(6066151976692092400)
XLA Ops:
  0.0 0.0 copy-start
  0.0 73.9 %shard_map.37 = f32[4096,128]{1,0:T(8,128)} custom-call(f32[4096,128]{1,0:T(8,128)} %rhs_hbm.1, bf16[4096,512]{1,0:T(8,128)(2,1)} %factors_hbm.1, f32[4,512,512]{2,1,0:T(8,128)} %diag_ref.1), custom_call_target="tpu_custom_call" | custom-call | tf_op jit(solution)/shard_map/pallas_call | solution.py:407
  73.9 0.0 copy-done
  73.9 3.1 %sub.3 = f32[4096,128]{1,0:T(8,128)} subtract(f32[4096,128]{1,0:T(8,128)S(1)} %copy-done, f32[4096,128]{1,0:T(8,128)} %shard_map.37) | non-fusion elementwise | flops 524288 | bytes 6291456 | tf_op jit(solution)/shard_map/sub | solution.py:441
Async XLA Ops:
  0.0 73.9 %copy-start = (f32[4096,128]{1,0:T(8,128)S(1)}, f32[4096,128]{1,0:T(8,128)}, u32[]{:S(2)}) copy-start(f32[4096,128]{1,0:T(8,128)} %rhs_hbm.1) | copy-start | bytes 6291460

commit v5 on v4

--- a/solution.py
+++ b/solution.py
@@ -107,7 +107,8 @@
             extra_copy(g, d).start()
         return carry
 
-    lax.fori_loop(0, n_extra, extra_start, 0)
+    waits = jnp.logical_and(owner, zone > 0)
+    lax.fori_loop(0, jnp.where(waits, 0, n_extra), extra_start, 0)
     diag_copy.wait()
     work_copy.wait()
     panel_own.wait()
@@ -326,6 +327,8 @@
                         update(j, q)
 
         hand_on(t + 1)
+        if t == 0:
+            lax.fori_loop(0, jnp.where(waits, n_extra, 0), extra_start, 0)
 
     def last_copy(q):
         target = jnp.where(zone > 0, zone - 1, 0) * side

time: 77.2 us -> 74.2 us (0.961)
  Pallas kernels: 73.9 us -> 71 us
    pallas_call x1, Pallas kernels: 73.9 us -> 71 us  [body(): pl.pallas_call(functools.partial(kernel, n_row, n_col, steps, block), out...]
where the time goes in v5:
time: 74.2 us; the launch traced here: 74.1 us
  Pallas kernels  71 us (96%)
  other arithmetic  3.12 us (4%)
    pallas_call x1, Pallas kernels, body(): pl.pallas_call(functools.partial(kernel, n_row, n_col, steps, block), out...  71 us
    sub x1, other arithmetic, body(): return rhs - taken  3.12 us

profile of v5, /device:TPU:0, one launch (start us, length us, event | category | flops | bytes accessed | tf_op | source)
XLA Modules:
  0.0 74.1 jit_solution(13343028671795312182)
XLA Ops:
  0.0 0.0 copy-start
  0.0 71.0 %shard_map.37 = f32[4096,128]{1,0:T(8,128)} custom-call(f32[4096,128]{1,0:T(8,128)} %rhs_hbm.1, bf16[4096,512]{1,0:T(8,128)(2,1)} %factors_hbm.1, f32[4,512,512]{2,1,0:T(8,128)} %diag_ref.1), custom_call_target="tpu_custom_call" | custom-call | tf_op jit(solution)/shard_map/pallas_call | solution.py:410
  71.0 0.0 copy-done
  71.0 3.1 %sub.3 = f32[4096,128]{1,0:T(8,128)} subtract(f32[4096,128]{1,0:T(8,128)S(1)} %copy-done, f32[4096,128]{1,0:T(8,128)} %shard_map.37) | non-fusion elementwise | flops 524288 | bytes 6291456 | tf_op jit(solution)/shard_map/sub | solution.py:444
Async XLA Ops:
  0.0 71.0 %copy-start = (f32[4096,128]{1,0:T(8,128)S(1)}, f32[4096,128]{1,0:T(8,128)}, u32[]{:S(2)}) copy-start(f32[4096,128]{1,0:T(8,128)} %rhs_hbm.1) | copy-start | bytes 6291460

commit v6 on v5

--- a/solution.py
+++ b/solution.py
@@ -334,8 +334,7 @@
         target = jnp.where(zone > 0, zone - 1, 0) * side
         return remote(last.at[part(q)], solved.at[zone, part(q)], s_last.at[q], s_recv.at[zone, q], col=target)
 
-    @pl.when(owner)
-    def _():
+    def solve_last():
         high, low = split(work[...])
         for q in range(PARTS):
             value = solve(up_hi, up_lo, high, low, q)
@@ -346,9 +345,11 @@
             def _():
                 last_copy(q).start()
 
+    pl.when(jnp.logical_and(owner, zone > 0))(solve_last)
     first_products()
     lax.fori_loop(0, n_swap, second, 0)
     lax.fori_loop(0, n_extra, extra_hand_on, 0)
+    pl.when(jnp.logical_and(owner, zone == 0))(solve_last)
     lax.fori_loop(0, n_extra, extra_product, 0)
     lax.fori_loop(0, n_swap, third, 0)
 

time: 74.2 us -> 73.6 us (level)
  no operation moved by 1% of the time
where the time goes in v6:
time: 73.6 us; the launch traced here: 73.5 us
  Pallas kernels  70.3 us (96%)
  other arithmetic  3.12 us (4%)
    pallas_call x1, Pallas kernels, body(): pl.pallas_call(functools.partial(kernel, n_row, n_col, steps, block), out...  70.3 us
    sub x1, other arithmetic, body(): return rhs - taken  3.12 us

profile of v6, /device:TPU:0, one launch (start us, length us, event | category | flops | bytes accessed | tf_op | source)
XLA Modules:
  0.0 73.5 jit_solution(12051049518089835661)
XLA Ops:
  0.0 0.0 copy-start
  0.0 70.3 %shard_map.37 = f32[4096,128]{1,0:T(8,128)} custom-call(f32[4096,128]{1,0:T(8,128)} %rhs_hbm.1, bf16[4096,512]{1,0:T(8,128)(2,1)} %factors_hbm.1, f32[4,512,512]{2,1,0:T(8,128)} %diag_ref.1), custom_call_target="tpu_custom_call" | custom-call | tf_op jit(solution)/shard_map/pallas_call | solution.py:411
  70.3 0.0 copy-done
  70.3 3.1 %sub.3 = f32[4096,128]{1,0:T(8,128)} subtract(f32[4096,128]{1,0:T(8,128)S(1)} %copy-done, f32[4096,128]{1,0:T(8,128)} %shard_map.37) | non-fusion elementwise | flops 524288 | bytes 6291456 | tf_op jit(solution)/shard_map/sub | solution.py:445
Async XLA Ops:
  0.0 70.3 %copy-start = (f32[4096,128]{1,0:T(8,128)S(1)}, f32[4096,128]{1,0:T(8,128)}, u32[]{:S(2)}) copy-start(f32[4096,128]{1,0:T(8,128)} %rhs_hbm.1) | copy-start | bytes 6291460

commit v7 on v6

--- a/solution.py
+++ b/solution.py
@@ -223,9 +223,9 @@
         return carry
 
     def second(m, carry):
-        @pl.when(m + 2 < n_swap)
-        def _():
-            first(m + 2, 0)
+        @pl.when(m + 1 < n_swap)
+        def _():
+            first(m + 1, 0)
 
         own1[m] = dot(factors_ref[span(m)], gathered[core])
         one_copy(m).wait_recv()
@@ -293,7 +293,6 @@
                 piece = gathered.at[source % 2, part(q), pl.ds(pl.multiple_of((source // 2) * width, width), width)]
                 remote(piece, piece, g_local.at[q], g_recv.at[source, q], row=source).wait_recv()
         first(0, 0)
-        first(1, 0)
 
     for t in range(steps):
         j = slot(t)

time: 73.6 us -> 73.1 us (level)
  no operation moved by 1% of the time
where the time goes in v7:
time: 73.1 us; the launch traced here: 72.9 us
  Pallas kernels  69.8 us (95%)
  other arithmetic  3.12 us (4%)
    pallas_call x1, Pallas kernels, body(): pl.pallas_call(functools.partial(kernel, n_row, n_col, steps, block), out...  69.8 us
    sub x1, other arithmetic, body(): return rhs - taken  3.12 us

profile of v7, /device:TPU:0, one launch (start us, length us, event | category | flops | bytes accessed | tf_op | source)
XLA Modules:
  0.0 72.9 jit_solution(5406840195497656402)
XLA Ops:
  0.0 0.0 copy-start
  0.0 69.8 %shard_map.37 = f32[4096,128]{1,0:T(8,128)} custom-call(f32[4096,128]{1,0:T(8,128)} %rhs_hbm.1, bf16[4096,512]{1,0:T(8,128)(2,1)} %factors_hbm.1, f32[4,512,512]{2,1,0:T(8,128)} %diag_ref.1), custom_call_target="tpu_custom_call" | custom-call | tf_op jit(solution)/shard_map/pallas_call | solution.py:410
  69.8 0.0 copy-done
  69.8 3.1 %sub.3 = f32[4096,128]{1,0:T(8,128)} subtract(f32[4096,128]{1,0:T(8,128)S(1)} %copy-done, f32[4096,128]{1,0:T(8,128)} %shard_map.37) | non-fusion elementwise | flops 524288 | bytes 6291456 | tf_op jit(solution)/shard_map/sub | solution.py:444
Async XLA Ops:
  0.0 69.8 %copy-start = (f32[4096,128]{1,0:T(8,128)S(1)}, f32[4096,128]{1,0:T(8,128)}, u32[]{:S(2)}) copy-start(f32[4096,128]{1,0:T(8,128)} %rhs_hbm.1) | copy-start | bytes 6291460
